TPU v7x, 32 devices: a whole 2x2x4 slice. The times are simulated.
32 devices in a mesh: dom: 16 (over z, y, x), chan: 2 (over core).
Axes of the slice: x: 2, y: 2, z: 4, core: 2. Of those that a mesh axis runs over, the one named last changes fastest.
Arguments:
- features: bfloat16 [16384, 512], P('dom', 'chan'), may hold values from -6 to 6
- w_self: bfloat16 [512, 512], P('chan'), may hold values from -0.25 to 0.25
- w_neigh: bfloat16 [512, 512], P('chan'), may hold values from -1.5 to 1.5
- degrees: int32 [16384], P('dom'), may hold values from 16 to 48
- local_src: int32 [128], P('dom'), may hold values from 0 to 7
- local_dst: int32 [128], P('dom'), may hold values from 0 to 7
- local_tiles: bfloat16 [128, 128, 128], P('dom'), may hold values from 0 to 1, as said below
- remote_src: int32 [256], P('dom'), may hold values from 0 to 7
- remote_part: int32 [256, 1], P('dom'), may hold values from 0 to 15; in each aligned block of 16 rows (0 to 15, 16 to 31, ...) at most 2 rows name the same one
- remote_dst: int32 [256], P('dom'), may hold values from 0 to 7
- remote_tiles: bfloat16 [256, 128, 128], P('dom'), may hold values from 0 to 1, as said below
- cotangent: bfloat16 [16384, 512], P('dom', 'chan'), may hold values from -6 to 6
Outputs:
- output: bfloat16 [16384, 512], P('dom', 'chan')
- grad_self: float32 [512, 512], P('chan')
- grad_neigh: float32 [512, 512], P('chan')
- grad_features: bfloat16 [16384, 512], P('dom', 'chan')
Inputs may be any that keep to these rules, and one draw needn't show every extreme that they name: `remote_part`: among the 16 remote tiles of one partition each partition is named at most 2 times, a bound that some block reaches. `local_tiles`: every entry is 0 or 1. `remote_tiles`: every entry is 0 or 1.
All inputs are finite; a program needn't handle non-finite values.
Results may differ from a plain program's by a relative error of at most 0.015.
Values may be sent and summed in bfloat16 or wider, within the bound.
No kernel may reach another device: no remote copies, remote signals or barrier semaphores. Data moves between devices by JAX's collectives and lax.ppermute only.
A program may use at most 64 MiB of HBM per device.

v0:
```python
import math

import jax
import jax.numpy as jnp
from jax import lax
from jax.experimental import pallas as pl
from jax.experimental.pallas import tpu as pltpu
from jax.sharding import PartitionSpec as P


TILE = 128
CAP = 2
TAG_ROWS = 8
PAIR = CAP * TILE

F32 = jnp.float32
BF16 = jnp.bfloat16
I32 = jnp.int32
VMEM = pl.BlockSpec(memory_space=pltpu.VMEM)
SMEM = pl.BlockSpec(memory_space=pltpu.SMEM)
HBM = pl.BlockSpec(memory_space=pltpu.HBM)


def shape(dims, dtype):
    return jax.ShapeDtypeStruct(dims, dtype)


def call(kernel, outs, ins, scratch=(), flops=1 << 20, limit=16 * 1024 * 1024, nbytes=1 << 20):
    return pl.pallas_call(
        kernel,
        out_shape=tuple(out for _, out in outs),
        in_specs=[spec for spec, _ in ins],
        out_specs=tuple(spec for spec, _ in outs),
        scratch_shapes=list(scratch),
        compiler_params=pltpu.CompilerParams(vmem_limit_bytes=limit),
        cost_estimate=pl.CostEstimate(flops=flops, bytes_accessed=nbytes, transcendentals=0),
    )(*[array for _, array in ins])


def vmem(arrays):
    return [(VMEM, array) for array in arrays]


def smem(arrays):
    return [(SMEM, array) for array in arrays]


def dot_tn(a, b):
    return lax.dot_general(a, b, (((0,), (0,)), ((), ())), preferred_element_type=F32)


def dot_nn(a, b):
    return lax.dot_general(a, b, (((1,), (0,)), ((), ())), preferred_element_type=F32)


def dot_nt(a, b):
    return lax.dot_general(a, b, (((1,), (1,)), ((), ())), preferred_element_type=F32)


def block_at(number):
    return slice(number * TILE, (number + 1) * TILE)


def fill_slots(part, count, slots, tiles):
    for place in range(count.shape[0]):
        count[place] = 0
    for place in range(slots.shape[0]):
        slots[place] = -1
    for number in range(tiles):
        target = part[number]
        place = count[target]
        count[target] = place + 1
        slots[target * CAP + place] = number


def degree_columns(degrees):
    return jnp.transpose(degrees[...].astype(F32))


def place_tiles(outs, first, product, slots, tags):
    me = lax.axis_index("dom")
    row_at = lax.broadcasted_iota(I32, (TAG_ROWS, product.shape[2]), 0)
    for relative, out in enumerate(outs, first):
        target = me ^ relative
        marks = jnp.zeros((TAG_ROWS, product.shape[2]), F32)
        for place in range(CAP):
            number = slots[target * CAP + place]
            marks = jnp.where(row_at == place, tags[target * CAP + place].astype(F32), marks)

            @pl.when(number >= 0)
            def _():
                out[block_at(place), :] = product[number]

        out[PAIR:, :] = marks.astype(BF16)


def push_far_kernel(half, src_hbm, part_hbm, dst_hbm, feat_hbm, tiles_hbm, *refs):
    outs, (product, slots, tags) = refs[:half], refs[half : half + 3]
    src, part, dst, feat, tiles, count, sems = refs[half + 3 :]
    pairs = [
        (part_hbm, part),
        (dst_hbm, dst),
        (src_hbm, src),
        (feat_hbm, feat),
        (tiles_hbm, tiles),
    ]
    copies = [
        pltpu.make_async_copy(source, target, sems.at[number])
        for number, (source, target) in enumerate(pairs)
    ]
    for copy in copies:
        copy.start()
    copies[0].wait()
    copies[1].wait()
    fill_slots(part, count, slots, tiles.shape[0])
    for place in range(slots.shape[0]):
        number = slots[place]
        tags[place] = jnp.where(number >= 0, dst[jnp.maximum(number, 0)] + 1, 0)
    for copy in copies[2:]:
        copy.wait()
    for number in range(tiles.shape[0]):
        product[number] = dot_tn(tiles[number], feat[src[number]]).astype(BF16)
    place_tiles(outs, half, product, slots, tags)


def push_near_kernel(product, slots, tags, *outs):
    place_tiles(outs, 0, product, slots, tags)


def local_kernel(src, dst, feat, tiles, out):
    out[...] = jnp.zeros(out.shape, F32)
    for number in range(tiles.shape[0]):
        out[dst[number]] += dot_tn(tiles[number], feat[src[number]])


def rotate_kernel(first, second, out_first, out_second):
    shards = lax.axis_size("chan")
    me = lax.axis_index("chan")
    width = first.shape[1] // shards
    for own in range(shards):

        @pl.when(me == own)
        def _():
            cut = own * width
            for source, out in ((first, out_first), (second, out_second)):
                out[:, : source.shape[1] - cut] = source[:, cut:]
                if cut:
                    out[:, source.shape[1] - cut :] = source[:, :cut]


def read_tags(pairs, blocks, got):
    channels = pairs[0].shape[1]
    bits = blocks.bit_length()
    per_word = max(1, 24 // (bits * CAP))
    row_at = lax.broadcasted_iota(I32, (TAG_ROWS, channels), 0)
    unit = jnp.zeros((TAG_ROWS, channels), F32)
    for place in range(CAP):
        unit = jnp.where(row_at == place, float(1 << (bits * place)), unit)
    for first in range(0, len(pairs), per_word):
        members = range(first, min(first + per_word, len(pairs)))
        word = jnp.zeros((TAG_ROWS, channels), F32)
        for member in members:
            scale = float(1 << (bits * CAP * (member - first)))
            word = word + pairs[member][PAIR:, :].astype(F32) * (unit * scale)
        packed = jnp.max(jnp.sum(word, axis=0, keepdims=True)).astype(I32)
        for member in members:
            for place in range(CAP):
                shift = bits * (CAP * (member - first) + place)
                got[member * CAP + place] = ((packed >> shift) & (2**bits - 1)) - 1


def add_pairs(pairs, got, acc):
    for number, pair in enumerate(pairs):
        for place in range(CAP):
            block = got[number * CAP + place]

            @pl.when(block >= 0)
            def _():
                acc[block] += pair[block_at(place), :].astype(F32)


def relay_kernel(*refs):
    pairs, (dense, got, acc) = refs[:-3], refs[-3:]
    read_tags(pairs, acc.shape[0], got)
    acc[...] = jnp.zeros(acc.shape, F32)
    add_pairs(pairs, got, acc)
    dense[...] = acc[...].astype(BF16)


def project(block, mean, feat, w_self, w_neigh, at, shares):
    width = shares[0].shape[1]
    value = dot_nn(feat[block], w_self[...]) + dot_nn(mean, w_neigh[...])
    value = value.astype(BF16)
    for piece, share in enumerate(shares):
        share[at, :] = value[:, piece * width : (piece + 1) * width]


def mid_kernel(half, shards, *refs):
    pairs, rest = refs[:half], refs[half:]
    dense, local, feat, w_self, w_neigh, degrees, averaged, later = rest[:8]
    shares, (got, acc) = rest[8 : 8 + shards], rest[8 + shards :]
    read_tags(pairs, acc.shape[0], got)
    acc[...] = local[...] + dense[...].astype(F32)
    add_pairs(pairs, got, acc)
    divisor = degree_columns(degrees)
    count = averaged.shape[0] // TILE
    for block in range(count):
        at = block_at(block)
        mean = (acc[block] / divisor[:, block : block + 1]).astype(BF16)
        averaged[at, :] = mean
        project(block, mean, feat, w_self, w_neigh, at, shares)
    later[...] = acc[count:]


def later_mid_kernel(sums, feat, w_self, w_neigh, degrees, averaged, *shares):
    divisor = degree_columns(degrees)
    first = feat.shape[0] - sums.shape[0]
    for place in range(sums.shape[0]):
        block, at = first + place, block_at(place)
        mean = (sums[place] / divisor[:, block : block + 1]).astype(BF16)
        averaged[at, :] = mean
        project(block, mean, feat, w_self, w_neigh, at, shares)


def value_and_gate(shares, at):
    value = shares[0][at, :].astype(F32)
    for piece in shares[1:]:
        value = value + piece[at, :].astype(F32)
    return value, 1.0 / (1.0 + jnp.exp(-value))


def slopes_kernel(first, *refs):
    shares, cotangent, slopes = refs[:-2], refs[-2], refs[-1]
    for block in range(slopes.shape[0] // TILE):
        at = block_at(block)
        value, gate = value_and_gate(shares, at)
        slope = gate * (1.0 + value * (1.0 - gate))
        slopes[at, :] = (cotangent[block_at(first + block), :].astype(F32) * slope).astype(BF16)


def output_kernel(*refs):
    shares, output = refs[:-1], refs[-1]
    first, second = shares[: len(shares) // 2], shares[len(shares) // 2 :]
    count = first[0].shape[0] // TILE
    for block in range(output.shape[0] // TILE):
        value, gate = value_and_gate(second if block >= count else first, block_at(block % count))
        output[block_at(block), :] = (value * gate).astype(BF16)


def slopes_times(slopes, weights, at):
    width = slopes[0].shape[1]
    total = dot_nt(slopes[0][at, :], weights[:, :width])
    for piece in range(1, len(slopes)):
        columns = slice(piece * width, (piece + 1) * width)
        total = total + dot_nt(slopes[piece][at, :], weights[:, columns])
    return total


def back_kernel(first, w_neigh, degrees, *refs):
    slopes, back = refs[:-1], refs[-1]
    divisor = degree_columns(degrees)
    for place in range(back.shape[0]):
        block = first + place
        total = slopes_times(slopes, w_neigh, block_at(place))
        back[place] = (total / divisor[:, block : block + 1]).astype(BF16)


def with_block(chunks, block, action):
    count = chunks[0].shape[0]
    for number, chunk in enumerate(chunks):
        first = number * count

        @pl.when((block >= first) & (block < first + count))
        def _():
            action(chunk, block - first)


def spread_kernel(got, first, second, *outs):
    for number, out in enumerate(outs, 1):
        for place in range(CAP):

            def copy(chunk, block):
                out[block_at(place), :] = chunk[block]

            with_block((first, second), got[number * CAP + place], copy)


def grads_kernel(inner, feat, means, more_means, *refs):
    shards = lax.axis_size("chan")
    chunks, outs, whole = refs[: 2 * shards], refs[2 * shards : -1], refs[-1]
    channels = feat.shape[1]
    count, width = chunks[0].shape
    for piece in range(shards):
        columns = slice(piece * width, (piece + 1) * width)
        first, second = chunks[piece][...], chunks[shards + piece][...]
        whole[:channels, columns] = dot_tn(feat[:count, :], first) + dot_tn(
            feat[count:, :], second
        )
        whole[channels:, columns] = dot_tn(means[...], first) + dot_tn(more_means[...], second)
    me = lax.axis_index("dom") & (inner - 1)
    rows = outs[0].shape[0]
    for relative, out in enumerate(outs):
        for owner in range(inner):

            @pl.when((me ^ relative) == owner)
            def _():
                out[...] = whole[owner * rows : (owner + 1) * rows, :].astype(out.dtype)


def gather_sum_kernel(*refs):
    parts, out = refs[:-1], refs[-1]
    total = parts[0][...].astype(F32)
    for part in parts[1:]:
        total = total + part[...].astype(F32)
    out[...] = total.astype(BF16)


def place_rows(parts, out):
    me = lax.axis_index("dom") & (len(parts) - 1)
    rows = parts[0].shape[0]
    for relative, part in enumerate(parts):
        for owner in range(len(parts)):

            @pl.when((me ^ relative) == owner)
            def _():
                out[owner * rows : (owner + 1) * rows, :] = part[...]


def finish_grads_kernel(scale, *refs):
    parts, outs, whole = refs[:-3], refs[-3:-1], refs[-1]
    place_rows(parts, whole)
    shards = lax.axis_size("chan")
    me = lax.axis_index("chan")
    columns = whole.shape[1]
    channels = outs[0].shape[0]
    for own in range(shards):

        @pl.when(me == own)
        def _():
            cut = own * (columns // shards)
            for number, out in enumerate(outs):
                rows = slice(number * channels, (number + 1) * channels)
                out[:, cut:] = whole[rows, : columns - cut].astype(F32) * scale
                if cut:
                    out[:, :cut] = whole[rows, columns - cut :].astype(F32) * scale


def local_back_kernel(shards, src, dst, tiles, first, second, w_self, *refs):
    chunks, out, back = refs[: 2 * shards], refs[2 * shards], refs[2 * shards + 1]
    count = first.shape[0]
    back[:count] = first[...]
    back[count:] = second[...]
    for block in range(out.shape[0]):
        slopes = chunks[shards:] if block >= count else chunks[:shards]
        out[block] = slopes_times(slopes, w_self, block_at(block % count))
    for number in range(tiles.shape[0]):
        out[src[number]] += dot_nn(tiles[number], back[dst[number]])


def final_kernel(half, src, dst, slots, tiles, *refs):
    back, far, partial = refs[:2], refs[2:4], refs[4]
    near_rows, far_rows = refs[5 : half + 4], refs[half + 4 : 2 * half + 3]
    out, rows, acc = refs[2 * half + 3 :]
    me = lax.axis_index("dom")
    for relative in range(2 * half):
        target = me ^ relative
        shift = relative % half
        for place in range(CAP):
            number = slots[target * CAP + place]
            if shift:
                arrived = (near_rows if relative < half else far_rows)[shift - 1]

                @pl.when(number >= 0)
                def _():
                    rows[number] = arrived[block_at(place), :]
            else:
                held = jnp.where(number >= 0, dst[jnp.maximum(number, 0)], -1)

                def copy(chunk, block):
                    rows[number] = chunk[block]

                with_block(back if relative < half else far, held, copy)

    acc[...] = partial[...]
    for number in range(tiles.shape[0]):
        acc[src[number]] += dot_nn(tiles[number], rows[number])
    out[...] = acc[...].astype(BF16)


def swap(value, relative):
    count = lax.axis_size("dom")
    pairs = [(at, at ^ relative) for at in range(count)]
    return lax.ppermute(value, "dom", pairs)


def nearest_first(top, bottom=1):
    return sorted(range(bottom, top), key=lambda k: (k.bit_count(), -k))


def swap_all(values, first):
    out = [values[0]] + [None] * (len(values) - 1)
    for k in nearest_first(len(values)):
        out[k] = swap(values[k], k * first)
    return out


def around(value, shift):
    count = lax.axis_size("chan")
    pairs = [(at, (at + shift) % count) for at in range(count)]
    return lax.ppermute(value, "chan", pairs)


def per_device(
    features,
    w_self,
    w_neigh,
    degrees,
    local_src,
    local_dst,
    local_tiles,
    remote_src,
    remote_part,
    remote_dst,
    remote_tiles,
    cotangent,
):
    domains = lax.axis_size("dom")
    shards = lax.axis_size("chan")
    node_rows, channels = features.shape
    out_width = w_self.shape[1]
    own_width = out_width // shards
    blocks = node_rows // TILE
    n_remote = remote_tiles.shape[0]
    half = domains // 2
    early = max(1, half // 2)
    inner, outer_bits = inner_and_outer(domains)
    feat_blocks = features.reshape(blocks, TILE, channels)
    degree_rows = degrees.reshape(blocks, TILE)
    targets = remote_part[:, 0]
    block_shape = (blocks, TILE, channels)
    product_shape = (n_remote, TILE, channels)
    pair_shape = shape((PAIR + TAG_ROWS, channels), BF16)
    slot_shape = shape((domains * CAP,), I32)
    got_shape = shape((half * CAP,), I32)

    pushed = call(
        lambda *refs: push_far_kernel(half, *refs),
        [(VMEM, pair_shape)] * half
        + [(VMEM, shape(product_shape, BF16)), (SMEM, slot_shape), (SMEM, slot_shape)],
        [(HBM, a) for a in (remote_src, targets, remote_dst, feat_blocks, remote_tiles)],
        [pltpu.SMEM((n_remote,), I32)] * 3
        + [
            pltpu.VMEM(block_shape, BF16),
            pltpu.VMEM(remote_tiles.shape, BF16),
            pltpu.SMEM((domains,), I32),
            pltpu.SemaphoreType.DMA((5,)),
        ],
        limit=None,
    )
    far, (product, slots, tags) = pushed[:half], pushed[half:]
    relayed = swap_all(far, 1)
    near = call(
        push_near_kernel, [(VMEM, pair_shape)] * half, vmem([product]) + smem([slots, tags])
    )
    (local,) = call(
        local_kernel,
        [(VMEM, shape(block_shape, F32))],
        smem([local_src, local_dst]) + vmem([feat_blocks, local_tiles]),
    )
    own_self, own_neigh = call(
        rotate_kernel, [(VMEM, shape(w_self.shape, BF16))] * 2, vmem([w_self, w_neigh])
    )
    dense, got_far = call(
        relay_kernel,
        [(VMEM, shape(block_shape, BF16)), (SMEM, got_shape)],
        vmem(relayed),
        [pltpu.VMEM(block_shape, F32)],
    )
    crossed = swap(dense, half)
    direct = [near[0]] + [None] * (half - 1)
    for k in [*nearest_first(half, early), *nearest_first(early)]:
        direct[k] = swap(near[k], k)

    chunk_blocks = (blocks // 2, blocks - blocks // 2)
    chunk_rows = chunk_blocks[0] * TILE
    share_shape = shape((chunk_rows, own_width), BF16)
    mean_shape = shape((chunk_rows, channels), BF16)
    means, later, *shares, got_near = call(
        lambda *refs: mid_kernel(half, shards, *refs),
        [(VMEM, mean_shape), (VMEM, shape((chunk_blocks[1], TILE, channels), F32))]
        + [(VMEM, share_shape)] * shards
        + [(SMEM, got_shape)],
        vmem(direct + [crossed, local, feat_blocks, own_self, own_neigh, degree_rows]),
        [pltpu.VMEM(block_shape, F32)],
    )
    more_means, *more_shares = call(
        later_mid_kernel,
        [(VMEM, mean_shape)] + [(VMEM, share_shape)] * shards,
        vmem([later, feat_blocks, own_self, own_neigh, degree_rows]),
    )
    pieces, slopes, back, back_far = [], [], [], []
    for chunk, part in enumerate((shares, more_shares)):
        arrived = [around(part[k], k) for k in range(1, shards)]
        pieces += [part[0], *arrived]
    for chunk in range(2):
        (own,) = call(
            lambda *refs: slopes_kernel(chunk * chunk_blocks[0], *refs),
            [(VMEM, share_shape)],
            vmem(pieces[chunk * shards : (chunk + 1) * shards] + [cotangent]),
        )
        slopes += [own] + [around(own, shards - k) for k in range(1, shards)]
    for chunk in range(2):
        (rows,) = call(
            lambda *refs: back_kernel(chunk * chunk_blocks[0], *refs),
            [(VMEM, shape((chunk_blocks[chunk], TILE, channels), BF16))],
            vmem([own_neigh, degree_rows] + slopes[chunk * shards : (chunk + 1) * shards]),
        )
        back.append(rows)
        back_far.append(swap(rows, half))
    returning = shape((PAIR, channels), BF16)
    near_out = call(spread_kernel, [(VMEM, returning)] * (half - 1), smem([got_near]) + vmem(back))
    near_back = swap_all([None, *near_out], 1)[1:]

    rows_inner = 2 * channels // inner
    terms = call(
        lambda *refs: grads_kernel(inner, *refs),
        [(VMEM, shape((rows_inner, out_width), F32))]
        + [(VMEM, shape((rows_inner, out_width), BF16))] * (inner - 1),
        vmem([features, means, more_means] + slopes),
        [pltpu.VMEM((2 * channels, out_width), F32)],
    )
    part_shape = shape((rows_inner, out_width), BF16)
    (total,) = call(gather_sum_kernel, [(VMEM, part_shape)], vmem(swap_all(terms, 1)))
    for bit in range(outer_bits):
        arrived = swap(total, inner << bit)
        (total,) = call(gather_sum_kernel, [(VMEM, part_shape)], vmem([total, arrived]))
    totals = swap_all([total] * inner, 1)
    scale = 1.0 / math.sqrt(float(node_rows * domains))
    grad_self, grad_neigh = call(
        lambda *refs: finish_grads_kernel(scale, *refs),
        [(VMEM, shape((channels, out_width), F32))] * 2,
        vmem(totals),
        [pltpu.VMEM((2 * channels, out_width), BF16)],
    )

    far_out = call(
        spread_kernel, [(VMEM, returning)] * (half - 1), smem([got_far]) + vmem(back_far)
    )
    far_back = swap_all([None, *far_out], 1)[1:]
    (partial,) = call(
        lambda *refs: local_back_kernel(shards, *refs),
        [(VMEM, shape(block_shape, F32))],
        smem([local_src, local_dst]) + vmem([local_tiles, *back, own_self] + slopes),
        [pltpu.VMEM(block_shape, BF16)],
    )
    (output,) = call(output_kernel, [(VMEM, shape((node_rows, own_width), BF16))], vmem(pieces))
    (grad_features,) = call(
        lambda *refs: final_kernel(half, *refs),
        [(VMEM, shape(block_shape, BF16))],
        smem([remote_src, remote_dst, slots])
        + vmem([remote_tiles, *back, *back_far, partial] + near_back + far_back),
        [pltpu.VMEM(product_shape, BF16), pltpu.VMEM(block_shape, F32)],
    )
    return (output, grad_self, grad_neigh, grad_features.reshape(node_rows, channels))


def inner_and_outer(domains):
    inner_bits = domains.bit_length() // 2
    return 1 << inner_bits, domains.bit_length() - 1 - inner_bits


def solution(mesh):
    in_specs = (
        P("dom", "chan"),
        P("chan", None),
        P("chan", None),
        P("dom"),
        P("dom"),
        P("dom"),
        P("dom", None, None),
        P("dom"),
        P("dom", None),
        P("dom"),
        P("dom", None, None),
        P("dom", "chan"),
    )
    out_specs = (P("dom", "chan"), P("chan", None), P("chan", None), P("dom", "chan"))
    return jax.shard_map(
        per_device, mesh=mesh, in_specs=in_specs, out_specs=out_specs, check_vma=False
    )
```

profile of v0, /device:TPU:0, one launch (start us, length us, event | category | flops | bytes accessed | tf_op | source)
XLA Modules:
  0.0 124.9 jit_solution(14046320526157457334)
XLA Ops:
  0.6 3.2 %shard_map.147 = (bf16[264,256]{1,0:T(8,128)(2,1)}, bf16[264,256]{1,0:T(8,128)(2,1)}, bf16[264,256]{1,0:T(8,128)(2,1)}, bf16[264,256]{1,0:T(8,128)(2,1)}, bf16[2...) custom-call(s32[16]{0:T(128)} %refs_0_.7, ...), custom_call_target="tpu_custom_call" | custom-call | flops 1048576 | bytes 1048576 | tf_op jit(solution)/shard_map/pallas_call | solution.py:29
  3.9 3.0 %collective-permute-start.7 = (bf16[264,256]{1,0:T(8,128)(2,1)}, bf16[264,256]{1,0:T(8,128)(2,1)S(1)}, u32[]{:S(2)}, u32[]{:S(2)}) collective-permute-start(bf16[264,256]{1,0:T(8,128)(2,1)} %get-tuple-element.67), channel_id=1, source_target_pairs={{0,2},{2,0},{4,6},{6,4},{8,10},{10,8},{12,14},{14,12},{16,18},{18,... | collective-permute-start | bytes 405512 | tf_op jit(solution)/shard_map/ppermute | solution.py:393
  8.5 2.0 %collective-permute-start.10 = (bf16[264,256]{1,0:T(8,128)(2,1)}, bf16[264,256]{1,0:T(8,128)(2,1)S(1)}, u32[]{:S(2)}, u32[]{:S(2)}) collective-permute-start(bf16[264,256]{1,0:T(8,128)(2,1)} %get-tuple-element.70), channel_id=1, source_target_pairs={{0,8},{2,10},{4,12},{6,14},{8,0},{10,2},{12,4},{14,6},{16,24},{18,... | collective-permute-start | bytes 405512 | tf_op jit(solution)/shard_map/ppermute | solution.py:393
  11.9 2.5 %collective-permute-start.12 = (bf16[264,256]{1,0:T(8,128)(2,1)}, bf16[264,256]{1,0:T(8,128)(2,1)S(1)}, u32[]{:S(2)}, u32[]{:S(2)}) collective-permute-start(bf16[264,256]{1,0:T(8,128)(2,1)} %get-tuple-element.72), channel_id=1, source_target_pairs={{0,12},{2,14},{4,8},{6,10},{8,4},{10,6},{12,0},{14,2},{16,28},{18,... | collective-permute-start | bytes 405512 | tf_op jit(solution)/shard_map/ppermute | solution.py:393
  16.2 3.2 %collective-permute-done.11.refs_5_ = bf16[264,256]{1,0:T(8,128)(2,1)S(1)} collective-permute-done((bf16[264,256]{1,0:T(8,128)(2,1)}, bf16[264,256]{1,0:T(8,128)(2,1)S(1)}, u32[]{:S(2)}, u32[]{:S(2)}) %collective-permute-start.11) | collective-permute-done | bytes 135200 | tf_op jit(solution)/shard_map/ppermute | solution.py:393
  19.4 2.9 %collective-permute-done.12.refs_6_ = bf16[264,256]{1,0:T(8,128)(2,1)S(1)} collective-permute-done((bf16[264,256]{1,0:T(8,128)(2,1)}, bf16[264,256]{1,0:T(8,128)(2,1)S(1)}, u32[]{:S(2)}, u32[]{:S(2)}) %collective-permute-start.12) | collective-permute-done | bytes 135200 | tf_op jit(solution)/shard_map/ppermute | solution.py:393
  22.3 1.9 %collective-permute-done.13.refs_7_ = bf16[264,256]{1,0:T(8,128)(2,1)S(1)} collective-permute-done((bf16[264,256]{1,0:T(8,128)(2,1)}, bf16[264,256]{1,0:T(8,128)(2,1)S(1)}, u32[]{:S(2)}, u32[]{:S(2)}) %collective-permute-start.13) | collective-permute-done | bytes 135200 | tf_op jit(solution)/shard_map/ppermute | solution.py:393
  26.1 2.6 %collective-permute-start.14 = (bf16[8,128,256]{2,1,0:T(8,128)(2,1)S(1)}, bf16[8,128,256]{2,1,0:T(8,128)(2,1)S(1)}, u32[]{:S(2)}, u32[]{:S(2)}) collective-permute-start(bf16[8,128,256]{2,1,0:T(8,128)(2,1)S(1)} %get-tuple-element.74), channel_id=1, source_target_pairs={{0,16},{2,18},{4,20},{6,22},{8,24},{10,26},{12,28},{14,30},{16,0},... | collective-permute-start | bytes 1572872 | tf_op jit(solution)/shard_map/ppermute | solution.py:393
  31.9 1.8 %collective-permute-start.2 = (bf16[264,256]{1,0:T(8,128)(2,1)S(1)}, bf16[264,256]{1,0:T(8,128)(2,1)S(1)}, u32[]{:S(2)}, u32[]{:S(2)}) collective-permute-start(bf16[264,256]{1,0:T(8,128)(2,1)S(1)} %get-tuple-element.61), channel_id=1, source_target_pairs={{0,6},{2,4},{4,2},{6,0},{8,14},{10,12},{12,10},{14,8},{16,22},{18,... | collective-permute-start | bytes 405512 | tf_op jit(solution)/shard_map/ppermute | solution.py:393
  35.3 2.0 %collective-permute-done.refs_1_ = bf16[264,256]{1,0:T(8,128)(2,1)S(1)} collective-permute-done((bf16[264,256]{1,0:T(8,128)(2,1)S(1)}, bf16[264,256]{1,0:T(8,128)(2,1)S(1)}, u32[]{:S(2)}, u32[]{:S(2)}) %collective-permute-start) | collective-permute-done | bytes 135200 | tf_op jit(solution)/shard_map/ppermute | solution.py:393
  41.7 2.3 %collective-permute-done.3.refs_4_ = bf16[264,256]{1,0:T(8,128)(2,1)S(1)} collective-permute-done((bf16[264,256]{1,0:T(8,128)(2,1)S(1)}, bf16[264,256]{1,0:T(8,128)(2,1)S(1)}, u32[]{:S(2)}, u32[]{:S(2)}) %collective-permute-start.3) | collective-permute-done | bytes 135200 | tf_op jit(solution)/shard_map/ppermute | solution.py:393
  44.0 10.3 %collective-permute-done.4.refs_5_ = bf16[264,256]{1,0:T(8,128)(2,1)S(1)} collective-permute-done((bf16[264,256]{1,0:T(8,128)(2,1)S(1)}, bf16[264,256]{1,0:T(8,128)(2,1)S(1)}, u32[]{:S(2)}, u32[]{:S(2)}) %collective-permute-start.4) | collective-permute-done | bytes 135200 | tf_op jit(solution)/shard_map/ppermute | solution.py:393
  55.2 2.1 %collective-permute-done.6.refs_7_ = bf16[264,256]{1,0:T(8,128)(2,1)S(1)} collective-permute-done((bf16[264,256]{1,0:T(8,128)(2,1)S(1)}, bf16[264,256]{1,0:T(8,128)(2,1)S(1)}, u32[]{:S(2)}, u32[]{:S(2)}) %collective-permute-start.6) | collective-permute-done | bytes 135200 | tf_op jit(solution)/shard_map/ppermute | solution.py:393
  70.1 2.5 %collective-permute-start.28 = (bf16[4,128,256]{2,1,0:T(8,128)(2,1)S(1)}, bf16[4,128,256]{2,1,0:T(8,128)(2,1)S(1)}, u32[]{:S(2)}, u32[]{:S(2)}) collective-permute-start(bf16[4,128,256]{2,1,0:T(8,128)(2,1)S(1)} %shard_map.163.refs_4_.second.refs_5_), channel_id=1, source_target_pairs={{0,16},{2,18},{4,20},{6,22},{8,24},{10,26},{12,28},{14,30},{16,0},... | collective-permute-start | bytes 786440 | tf_op jit(solution)/shard_map/ppermute | solution.py:393
  75.7 4.7 %collective-permute-done.30.refs_10_ = bf16[256,256]{1,0:T(8,128)(2,1)S(1)} collective-permute-done((bf16[256,256]{1,0:T(8,128)(2,1)S(1)}, bf16[256,256]{1,0:T(8,128)(2,1)S(1)}, u32[]{:S(2)}, u32[]{:S(2)}) %collective-permute-start.30) | collective-permute-done | bytes 131104 | tf_op jit(solution)/shard_map/ppermute | solution.py:393
  80.4 2.9 %collective-permute-start.33 = (bf16[256,256]{1,0:T(8,128)(2,1)S(1)}, bf16[256,256]{1,0:T(8,128)(2,1)S(1)}, u32[]{:S(2)}, u32[]{:S(2)}) collective-permute-start(bf16[256,256]{1,0:T(8,128)(2,1)S(1)} %get-tuple-element.95), channel_id=1, source_target_pairs={{0,10},{2,8},{4,14},{6,12},{8,2},{10,0},{12,6},{14,4},{16,26},{18,... | collective-permute-start | bytes 393224 | tf_op jit(solution)/shard_map/ppermute | solution.py:393
  84.8 3.4 %collective-permute-start.34 = (bf16[256,256]{1,0:T(8,128)(2,1)S(1)}, bf16[256,256]{1,0:T(8,128)(2,1)S(1)}, u32[]{:S(2)}, u32[]{:S(2)}) collective-permute-start(bf16[256,256]{1,0:T(8,128)(2,1)S(1)} %get-tuple-element.96), channel_id=1, source_target_pairs={{0,12},{2,14},{4,8},{6,10},{8,4},{10,6},{12,0},{14,2},{16,28},{18,... | collective-permute-start | bytes 393224 | tf_op jit(solution)/shard_map/ppermute | solution.py:393
  89.7 4.5 %collective-permute-done.28.second.refs_7_ = bf16[4,128,256]{2,1,0:T(8,128)(2,1)S(1)} collective-permute-done((bf16[4,128,256]{2,1,0:T(8,128)(2,1)S(1)}, bf16[4,128,256]{2,1,0:T(8,128)(2,1)S(1)}, u32[]{:S(2)}, u32[]{:S(2)}) %collective-permute-start.28) | collective-permute-done | bytes 262176 | tf_op jit(solution)/shard_map/ppermute | solution.py:393
  94.9 1.6 %collective-permute-done.32.refs_12_ = bf16[256,256]{1,0:T(8,128)(2,1)S(1)} collective-permute-done((bf16[256,256]{1,0:T(8,128)(2,1)S(1)}, bf16[256,256]{1,0:T(8,128)(2,1)S(1)}, u32[]{:S(2)}, u32[]{:S(2)}) %collective-permute-start.32) | collective-permute-done | bytes 131104 | tf_op jit(solution)/shard_map/ppermute | solution.py:393
  97.4 2.4 %collective-permute-done.33.refs_13_ = bf16[256,256]{1,0:T(8,128)(2,1)S(1)} collective-permute-done((bf16[256,256]{1,0:T(8,128)(2,1)S(1)}, bf16[256,256]{1,0:T(8,128)(2,1)S(1)}, u32[]{:S(2)}, u32[]{:S(2)}) %collective-permute-start.33) | collective-permute-done | bytes 131104 | tf_op jit(solution)/shard_map/ppermute | solution.py:393
  100.6 5.2 %collective-permute-done.34.refs_14_ = bf16[256,256]{1,0:T(8,128)(2,1)S(1)} collective-permute-done((bf16[256,256]{1,0:T(8,128)(2,1)S(1)}, bf16[256,256]{1,0:T(8,128)(2,1)S(1)}, u32[]{:S(2)}, u32[]{:S(2)}) %collective-permute-start.34) | collective-permute-done | bytes 131104 | tf_op jit(solution)/shard_map/ppermute | solution.py:393
  107.6 2.3 %collective-permute-start.40 = (bf16[256,256]{1,0:T(8,128)(2,1)S(1)}, bf16[256,256]{1,0:T(8,128)(2,1)S(1)}, u32[]{:S(2)}, u32[]{:S(2)}) collective-permute-start(bf16[256,256]{1,0:T(8,128)(2,1)S(1)} %get-tuple-element.103), channel_id=1, source_target_pairs={{0,10},{2,8},{4,14},{6,12},{8,2},{10,0},{12,6},{14,4},{16,26},{18,... | collective-permute-start | bytes 393224 | tf_op jit(solution)/shard_map/ppermute | solution.py:393
  110.4 3.2 %collective-permute-start.42 = (bf16[256,256]{1,0:T(8,128)(2,1)S(1)}, bf16[256,256]{1,0:T(8,128)(2,1)S(1)}, u32[]{:S(2)}, u32[]{:S(2)}) collective-permute-start(bf16[256,256]{1,0:T(8,128)(2,1)S(1)} %get-tuple-element.105), channel_id=1, source_target_pairs={{0,14},{2,12},{4,10},{6,8},{8,6},{10,4},{12,2},{14,0},{16,30},{18,... | collective-permute-start | bytes 393224 | tf_op jit(solution)/shard_map/ppermute | solution.py:393
  121.0 2.2 %shard_map.167 = bf16[8,128,256]{2,1,0:T(8,128)(2,1)} custom-call(s32[16]{0:T(128)S(1)} %copy-done.12, s32[16]{0:T(128)S(1)} %copy-done.13, s32[32]{0:T(128)S(1)} %copy-done.9, bf16[16,128,128]{2,1,0:T(8,128)(2,1)S(1)} %copy-done.1, bf16[4,128,256]{2,1,0:T(8,128)(2,1)S(1)} %shard_map.162.refs_3_.first.refs_4_, ...), custom_call_target="tpu_custom_call" | custom-call | flops 1048576 | bytes 1048576 | tf_op jit(solution)/shard_map/pallas_call | solution.py:29
  (113 shorter events, 49.1 us)
Async XLA Ops:
  10.5 8.9 %collective-permute-start.11 = (bf16[264,256]{1,0:T(8,128)(2,1)}, bf16[264,256]{1,0:T(8,128)(2,1)S(1)}, u32[]{:S(2)}, u32[]{:S(2)}) collective-permute-start(bf16[264,256]{1,0:T(8,128)(2,1)} %get-tuple-element.71), channel_id=1, source_target_pairs={{0,10},{2,8},{4,14},{6,12},{8,2},{10,0},{12,6},{14,4},{16,26},{18,... | collective-permute-start | bytes 405512 | tf_op jit(solution)/shard_map/ppermute | solution.py:393
  11.9 10.4 %collective-permute-start.12 = (bf16[264,256]{1,0:T(8,128)(2,1)}, bf16[264,256]{1,0:T(8,128)(2,1)S(1)}, u32[]{:S(2)}, u32[]{:S(2)}) collective-permute-start(bf16[264,256]{1,0:T(8,128)(2,1)} %get-tuple-element.72), channel_id=1, source_target_pairs={{0,12},{2,14},{4,8},{6,10},{8,4},{10,6},{12,0},{14,2},{16,28},{18,... | collective-permute-start | bytes 405512 | tf_op jit(solution)/shard_map/ppermute | solution.py:393
  14.4 9.8 %collective-permute-start.13 = (bf16[264,256]{1,0:T(8,128)(2,1)}, bf16[264,256]{1,0:T(8,128)(2,1)S(1)}, u32[]{:S(2)}, u32[]{:S(2)}) collective-permute-start(bf16[264,256]{1,0:T(8,128)(2,1)} %get-tuple-element.73), channel_id=1, source_target_pairs={{0,14},{2,12},{4,10},{6,8},{8,6},{10,4},{12,2},{14,0},{16,30},{18,... | collective-permute-start | bytes 405512 | tf_op jit(solution)/shard_map/ppermute | solution.py:393
  26.1 31.2 %collective-permute-start.14 = (bf16[8,128,256]{2,1,0:T(8,128)(2,1)S(1)}, bf16[8,128,256]{2,1,0:T(8,128)(2,1)S(1)}, u32[]{:S(2)}, u32[]{:S(2)}) collective-permute-start(bf16[8,128,256]{2,1,0:T(8,128)(2,1)S(1)} %get-tuple-element.74), channel_id=1, source_target_pairs={{0,16},{2,18},{4,20},{6,22},{8,24},{10,26},{12,28},{14,30},{16,0},... | collective-permute-start | bytes 1572872 | tf_op jit(solution)/shard_map/ppermute | solution.py:393
  33.7 10.2 %collective-permute-start.3 = (bf16[264,256]{1,0:T(8,128)(2,1)S(1)}, bf16[264,256]{1,0:T(8,128)(2,1)S(1)}, u32[]{:S(2)}, u32[]{:S(2)}) collective-permute-start(bf16[264,256]{1,0:T(8,128)(2,1)S(1)} %get-tuple-element.62), channel_id=1, source_target_pairs={{0,8},{2,10},{4,12},{6,14},{8,0},{10,2},{12,4},{14,6},{16,24},{18,... | collective-permute-start | bytes 405512 | tf_op jit(solution)/shard_map/ppermute | solution.py:393
  37.3 17.0 %collective-permute-start.4 = (bf16[264,256]{1,0:T(8,128)(2,1)S(1)}, bf16[264,256]{1,0:T(8,128)(2,1)S(1)}, u32[]{:S(2)}, u32[]{:S(2)}) collective-permute-start(bf16[264,256]{1,0:T(8,128)(2,1)S(1)} %get-tuple-element.63), channel_id=1, source_target_pairs={{0,10},{2,8},{4,14},{6,12},{8,2},{10,0},{12,6},{14,4},{16,26},{18,... | collective-permute-start | bytes 405512 | tf_op jit(solution)/shard_map/ppermute | solution.py:393
  37.3 17.9 %collective-permute-start.5 = (bf16[264,256]{1,0:T(8,128)(2,1)S(1)}, bf16[264,256]{1,0:T(8,128)(2,1)S(1)}, u32[]{:S(2)}, u32[]{:S(2)}) collective-permute-start(bf16[264,256]{1,0:T(8,128)(2,1)S(1)} %get-tuple-element.64), channel_id=1, source_target_pairs={{0,12},{2,14},{4,8},{6,10},{8,4},{10,6},{12,0},{14,2},{16,28},{18,... | collective-permute-start | bytes 405512 | tf_op jit(solution)/shard_map/ppermute | solution.py:393
  39.3 17.9 %collective-permute-start.6 = (bf16[264,256]{1,0:T(8,128)(2,1)S(1)}, bf16[264,256]{1,0:T(8,128)(2,1)S(1)}, u32[]{:S(2)}, u32[]{:S(2)}) collective-permute-start(bf16[264,256]{1,0:T(8,128)(2,1)S(1)} %get-tuple-element.65), channel_id=1, source_target_pairs={{0,14},{2,12},{4,10},{6,8},{8,6},{10,4},{12,2},{14,0},{16,30},{18,... | collective-permute-start | bytes 405512 | tf_op jit(solution)/shard_map/ppermute | solution.py:393
  64.3 8.3 %collective-permute-start.20 = (bf16[128,512]{1,0:T(8,128)(2,1)S(1)}, bf16[128,512]{1,0:T(8,128)(2,1)S(1)}, u32[]{:S(2)}, u32[]{:S(2)}) collective-permute-start(bf16[128,512]{1,0:T(8,128)(2,1)S(1)} %get-tuple-element.86), channel_id=1, source_target_pairs={{0,4},{2,6},{4,0},{6,2},{8,12},{10,14},{12,8},{14,10},{16,20},{18,... | collective-permute-start | bytes 393224 | tf_op jit(solution)/shard_map/ppermute | solution.py:393
  69.7 18.9 %collective-permute-start.27 = (bf16[4,128,256]{2,1,0:T(8,128)(2,1)S(1)}, bf16[4,128,256]{2,1,0:T(8,128)(2,1)S(1)}, u32[]{:S(2)}, u32[]{:S(2)}) collective-permute-start(bf16[4,128,256]{2,1,0:T(8,128)(2,1)S(1)} %shard_map.162.refs_3_.first.refs_4_), channel_id=1, source_target_pairs={{0,16},{2,18},{4,20},{6,22},{8,24},{10,26},{12,28},{14,30},{16,0},... | collective-permute-start | bytes 786440 | tf_op jit(solution)/shard_map/ppermute | solution.py:393
  70.1 24.0 %collective-permute-start.28 = (bf16[4,128,256]{2,1,0:T(8,128)(2,1)S(1)}, bf16[4,128,256]{2,1,0:T(8,128)(2,1)S(1)}, u32[]{:S(2)}, u32[]{:S(2)}) collective-permute-start(bf16[4,128,256]{2,1,0:T(8,128)(2,1)S(1)} %shard_map.163.refs_4_.second.refs_5_), channel_id=1, source_target_pairs={{0,16},{2,18},{4,20},{6,22},{8,24},{10,26},{12,28},{14,30},{16,0},... | collective-permute-start | bytes 786440 | tf_op jit(solution)/shard_map/ppermute | solution.py:393
  75.6 9.2 %collective-permute-start.22 = (bf16[128,512]{1,0:T(8,128)(2,1)S(1)}, bf16[128,512]{1,0:T(8,128)(2,1)S(1)}, u32[]{:S(2)}, u32[]{:S(2)}) collective-permute-start(bf16[128,512]{1,0:T(8,128)(2,1)S(1)} %shard_map.158.refs_0_), channel_id=1, source_target_pairs={{0,8},{2,10},{4,12},{6,14},{8,0},{10,2},{12,4},{14,6},{16,24},{18,... | collective-permute-start | bytes 393224 | tf_op jit(solution)/shard_map/ppermute | solution.py:393
  80.4 16.2 %collective-permute-start.32 = (bf16[256,256]{1,0:T(8,128)(2,1)S(1)}, bf16[256,256]{1,0:T(8,128)(2,1)S(1)}, u32[]{:S(2)}, u32[]{:S(2)}) collective-permute-start(bf16[256,256]{1,0:T(8,128)(2,1)S(1)} %get-tuple-element.94), channel_id=1, source_target_pairs={{0,8},{2,10},{4,12},{6,14},{8,0},{10,2},{12,4},{14,6},{16,24},{18,... | collective-permute-start | bytes 393224 | tf_op jit(solution)/shard_map/ppermute | solution.py:393
  80.4 19.4 %collective-permute-start.33 = (bf16[256,256]{1,0:T(8,128)(2,1)S(1)}, bf16[256,256]{1,0:T(8,128)(2,1)S(1)}, u32[]{:S(2)}, u32[]{:S(2)}) collective-permute-start(bf16[256,256]{1,0:T(8,128)(2,1)S(1)} %get-tuple-element.95), channel_id=1, source_target_pairs={{0,10},{2,8},{4,14},{6,12},{8,2},{10,0},{12,6},{14,4},{16,26},{18,... | collective-permute-start | bytes 393224 | tf_op jit(solution)/shard_map/ppermute | solution.py:393
  84.8 21.0 %collective-permute-start.34 = (bf16[256,256]{1,0:T(8,128)(2,1)S(1)}, bf16[256,256]{1,0:T(8,128)(2,1)S(1)}, u32[]{:S(2)}, u32[]{:S(2)}) collective-permute-start(bf16[256,256]{1,0:T(8,128)(2,1)S(1)} %get-tuple-element.96), channel_id=1, source_target_pairs={{0,12},{2,14},{4,8},{6,10},{8,4},{10,6},{12,0},{14,2},{16,28},{18,... | collective-permute-start | bytes 393224 | tf_op jit(solution)/shard_map/ppermute | solution.py:393
  88.6 19.0 %collective-permute-start.35 = (bf16[256,256]{1,0:T(8,128)(2,1)S(1)}, bf16[256,256]{1,0:T(8,128)(2,1)S(1)}, u32[]{:S(2)}, u32[]{:S(2)}) collective-permute-start(bf16[256,256]{1,0:T(8,128)(2,1)S(1)} %get-tuple-element.97), channel_id=1, source_target_pairs={{0,14},{2,12},{4,10},{6,8},{8,6},{10,4},{12,2},{14,0},{16,30},{18,... | collective-permute-start | bytes 393224 | tf_op jit(solution)/shard_map/ppermute | solution.py:393
  94.1 13.5 %collective-permute-start.23 = (bf16[128,512]{1,0:T(8,128)(2,1)S(1)}, bf16[128,512]{1,0:T(8,128)(2,1)S(1)}, u32[]{:S(2)}, u32[]{:S(2)}) collective-permute-start(bf16[128,512]{1,0:T(8,128)(2,1)S(1)} %shard_map.159.refs_0_), channel_id=1, source_target_pairs={{0,16},{2,18},{4,20},{6,22},{8,24},{10,26},{12,28},{14,30},{16,0},... | collective-permute-start | bytes 393224 | tf_op jit(solution)/shard_map/ppermute | solution.py:393
  96.6 13.4 %collective-permute-start.36 = (bf16[256,256]{1,0:T(8,128)(2,1)S(1)}, bf16[256,256]{1,0:T(8,128)(2,1)S(1)}, u32[]{:S(2)}, u32[]{:S(2)}) collective-permute-start(bf16[256,256]{1,0:T(8,128)(2,1)S(1)} %get-tuple-element.99), channel_id=1, source_target_pairs={{0,2},{2,0},{4,6},{6,4},{8,10},{10,8},{12,14},{14,12},{16,18},{18,... | collective-permute-start | bytes 393224 | tf_op jit(solution)/shard_map/ppermute | solution.py:393
  99.8 10.6 %collective-permute-start.37 = (bf16[256,256]{1,0:T(8,128)(2,1)S(1)}, bf16[256,256]{1,0:T(8,128)(2,1)S(1)}, u32[]{:S(2)}, u32[]{:S(2)}) collective-permute-start(bf16[256,256]{1,0:T(8,128)(2,1)S(1)} %get-tuple-element.100), channel_id=1, source_target_pairs={{0,4},{2,6},{4,0},{6,2},{8,12},{10,14},{12,8},{14,10},{16,20},{18,... | collective-permute-start | bytes 393224 | tf_op jit(solution)/shard_map/ppermute | solution.py:393
  107.6 9.2 %collective-permute-start.40 = (bf16[256,256]{1,0:T(8,128)(2,1)S(1)}, bf16[256,256]{1,0:T(8,128)(2,1)S(1)}, u32[]{:S(2)}, u32[]{:S(2)}) collective-permute-start(bf16[256,256]{1,0:T(8,128)(2,1)S(1)} %get-tuple-element.103), channel_id=1, source_target_pairs={{0,10},{2,8},{4,14},{6,12},{8,2},{10,0},{12,6},{14,4},{16,26},{18,... | collective-permute-start | bytes 393224 | tf_op jit(solution)/shard_map/ppermute | solution.py:393
  110.0 11.0 %collective-permute-start.41 = (bf16[256,256]{1,0:T(8,128)(2,1)S(1)}, bf16[256,256]{1,0:T(8,128)(2,1)S(1)}, u32[]{:S(2)}, u32[]{:S(2)}) collective-permute-start(bf16[256,256]{1,0:T(8,128)(2,1)S(1)} %get-tuple-element.104), channel_id=1, source_target_pairs={{0,12},{2,14},{4,8},{6,10},{8,4},{10,6},{12,0},{14,2},{16,28},{18,... | collective-permute-start | bytes 393224 | tf_op jit(solution)/shard_map/ppermute | solution.py:393
  110.4 10.6 %collective-permute-start.42 = (bf16[256,256]{1,0:T(8,128)(2,1)S(1)}, bf16[256,256]{1,0:T(8,128)(2,1)S(1)}, u32[]{:S(2)}, u32[]{:S(2)}) collective-permute-start(bf16[256,256]{1,0:T(8,128)(2,1)S(1)} %get-tuple-element.105), channel_id=1, source_target_pairs={{0,14},{2,12},{4,10},{6,8},{8,6},{10,4},{12,2},{14,0},{16,30},{18,... | collective-permute-start | bytes 393224 | tf_op jit(solution)/shard_map/ppermute | solution.py:393
  113.6 9.7 %collective-permute-start.26 = (bf16[128,512]{1,0:T(8,128)(2,1)S(1)}, bf16[128,512]{1,0:T(8,128)(2,1)S(1)}, u32[]{:S(2)}, u32[]{:S(2)}) collective-permute-start(bf16[128,512]{1,0:T(8,128)(2,1)S(1)} %shard_map.160.refs_0_), channel_id=1, source_target_pairs={{0,6},{2,4},{4,2},{6,0},{8,14},{10,12},{12,10},{14,8},{16,22},{18,... | collective-permute-start | bytes 393224 | tf_op jit(solution)/shard_map/ppermute | solution.py:393
  114.7 9.0 %collective-permute-start.25 = (bf16[128,512]{1,0:T(8,128)(2,1)S(1)}, bf16[128,512]{1,0:T(8,128)(2,1)S(1)}, u32[]{:S(2)}, u32[]{:S(2)}) collective-permute-start(bf16[128,512]{1,0:T(8,128)(2,1)S(1)} %shard_map.160.refs_0_), channel_id=1, source_target_pairs={{0,4},{2,6},{4,0},{6,2},{8,12},{10,14},{12,8},{14,10},{16,20},{18,... | collective-permute-start | bytes 393224 | tf_op jit(solution)/shard_map/ppermute | solution.py:393
  (34 other events, 211.2 us)
where the time goes:
time: 125 us
  starting transfers between devices  52.9 us (42%)
  waiting for transfers between devices  51.6 us (41%)
  Pallas kernels  17.8 us (14%)
  local copies, waits for them, and re-layouts  1.62 us (1%)
    ppermute x39, starting transfers between devices, swap(): return lax.ppermute(value, 'dom', pairs)  51.6 us
    ppermute x39, waiting for transfers between devices, swap(): return lax.ppermute(value, 'dom', pairs)  49.8 us
    pallas_call x21, Pallas kernels, call(): pl.pallas_call(kernel, out_shape=tuple((out for _, out in outs)), in_spec...  17.8 us
  transfers between devices with their start and end apart: 43, of which 25 were waited for; matrix products, arithmetic and copies ran while one was open for 0% of the time, Pallas kernels for 8%

commit v1 on v0

--- a/solution.py
+++ b/solution.py
@@ -180,11 +180,13 @@
 
 
 def relay_kernel(*refs):
-    pairs, (dense, got, acc) = refs[:-3], refs[-3:]
+    pairs, (dense, more_dense, got, acc) = refs[:-4], refs[-4:]
     read_tags(pairs, acc.shape[0], got)
     acc[...] = jnp.zeros(acc.shape, F32)
     add_pairs(pairs, got, acc)
-    dense[...] = acc[...].astype(BF16)
+    count = dense.shape[0]
+    dense[...] = acc[:count].astype(BF16)
+    more_dense[...] = acc[count:].astype(BF16)
 
 
 def project(block, mean, feat, w_self, w_neigh, at, shares):
@@ -200,10 +202,11 @@
     dense, local, feat, w_self, w_neigh, degrees, averaged, later = rest[:8]
     shares, (got, acc) = rest[8 : 8 + shards], rest[8 + shards :]
     read_tags(pairs, acc.shape[0], got)
-    acc[...] = local[...] + dense[...].astype(F32)
+    count = dense.shape[0]
+    acc[:count] = local[:count] + dense[...].astype(F32)
+    acc[count:] = local[count:]
     add_pairs(pairs, got, acc)
     divisor = degree_columns(degrees)
-    count = averaged.shape[0] // TILE
     for block in range(count):
         at = block_at(block)
         mean = (acc[block] / divisor[:, block : block + 1]).astype(BF16)
@@ -212,12 +215,13 @@
     later[...] = acc[count:]
 
 
-def later_mid_kernel(sums, feat, w_self, w_neigh, degrees, averaged, *shares):
+def later_mid_kernel(sums, dense, feat, w_self, w_neigh, degrees, averaged, *shares):
     divisor = degree_columns(degrees)
     first = feat.shape[0] - sums.shape[0]
     for place in range(sums.shape[0]):
         block, at = first + place, block_at(place)
-        mean = (sums[place] / divisor[:, block : block + 1]).astype(BF16)
+        total = sums[place] + dense[place].astype(F32)
+        mean = (total / divisor[:, block : block + 1]).astype(BF16)
         averaged[at, :] = mean
         project(block, mean, feat, w_self, w_neigh, at, shares)
 
@@ -470,18 +474,20 @@
     own_self, own_neigh = call(
         rotate_kernel, [(VMEM, shape(w_self.shape, BF16))] * 2, vmem([w_self, w_neigh])
     )
-    dense, got_far = call(
+    chunk_blocks = (blocks // 2, blocks - blocks // 2)
+    chunk_shapes = [(VMEM, shape((count, TILE, channels), BF16)) for count in chunk_blocks]
+    dense, more_dense, got_far = call(
         relay_kernel,
-        [(VMEM, shape(block_shape, BF16)), (SMEM, got_shape)],
+        [*chunk_shapes, (SMEM, got_shape)],
         vmem(relayed),
         [pltpu.VMEM(block_shape, F32)],
     )
     crossed = swap(dense, half)
+    more_crossed = swap(more_dense, half)
     direct = [near[0]] + [None] * (half - 1)
     for k in [*nearest_first(half, early), *nearest_first(early)]:
         direct[k] = swap(near[k], k)
 
-    chunk_blocks = (blocks // 2, blocks - blocks // 2)
     chunk_rows = chunk_blocks[0] * TILE
     share_shape = shape((chunk_rows, own_width), BF16)
     mean_shape = shape((chunk_rows, channels), BF16)
@@ -496,7 +502,7 @@
     more_means, *more_shares = call(
         later_mid_kernel,
         [(VMEM, mean_shape)] + [(VMEM, share_shape)] * shards,
-        vmem([later, feat_blocks, own_self, own_neigh, degree_rows]),
+        vmem([later, more_crossed, feat_blocks, own_self, own_neigh, degree_rows]),
     )
     pieces, slopes, back, back_far = [], [], [], []
     for chunk, part in enumerate((shares, more_shares)):

time: 125 us -> 121 us (0.968)
  waiting for transfers between devices: 51.6 us -> 34.4 us
  starting transfers between devices: 52.9 us -> 65.3 us
    ppermute x39 -> x40, waiting for transfers between devices: 49.8 us -> 32.6 us  [swap(): return lax.ppermute(value, 'dom', pairs)]
    ppermute x39 -> x40, starting transfers between devices: 51.6 us -> 64 us  [swap(): return lax.ppermute(value, 'dom', pairs)]
  transfers between devices with their start and end apart: 43 -> 44, of which waited for: 25 -> 16; matrix products, arithmetic and copies ran while one was open for 0% -> 0% of each run, Pallas kernels for 8% -> 10%
where the time goes in v1:
time: 121 us
  starting transfers between devices  65.3 us (54%)
  waiting for transfers between devices  34.4 us (28%)
  Pallas kernels  17.9 us (15%)
  local copies, waits for them, and re-layouts  1.96 us (2%)
    ppermute x40, starting transfers between devices, swap(): return lax.ppermute(value, 'dom', pairs)  64 us
    ppermute x40, waiting for transfers between devices, swap(): return lax.ppermute(value, 'dom', pairs)  32.6 us
    pallas_call x21, Pallas kernels, call(): pl.pallas_call(kernel, out_shape=tuple((out for _, out in outs)), in_spec...  17.9 us
  transfers between devices with their start and end apart: 44, of which 16 were waited for; matrix products, arithmetic and copies ran while one was open for 0% of the time, Pallas kernels for 10%

profile of v1, /device:TPU:0, one launch (start us, length us, event | category | flops | bytes accessed | tf_op | source)
XLA Modules:
  0.0 120.5 jit_solution(3699063190317739862)
XLA Ops:
  0.6 3.2 %shard_map.147 = (bf16[264,256]{1,0:T(8,128)(2,1)}, bf16[264,256]{1,0:T(8,128)(2,1)}, bf16[264,256]{1,0:T(8,128)(2,1)}, bf16[264,256]{1,0:T(8,128)(2,1)}, bf16[2...) custom-call(s32[16]{0:T(128)} %refs_0_.7, ...), custom_call_target="tpu_custom_call" | custom-call | flops 1048576 | bytes 1048576 | tf_op jit(solution)/shard_map/pallas_call | solution.py:29
  3.9 3.0 %collective-permute-start.7 = (bf16[264,256]{1,0:T(8,128)(2,1)}, bf16[264,256]{1,0:T(8,128)(2,1)S(1)}, u32[]{:S(2)}, u32[]{:S(2)}) collective-permute-start(bf16[264,256]{1,0:T(8,128)(2,1)} %get-tuple-element.68), channel_id=1, source_target_pairs={{0,2},{2,0},{4,6},{6,4},{8,10},{10,8},{12,14},{14,12},{16,18},{18,... | collective-permute-start | bytes 405512 | tf_op jit(solution)/shard_map/ppermute | solution.py:397
  8.5 2.0 %collective-permute-start.10 = (bf16[264,256]{1,0:T(8,128)(2,1)}, bf16[264,256]{1,0:T(8,128)(2,1)S(1)}, u32[]{:S(2)}, u32[]{:S(2)}) collective-permute-start(bf16[264,256]{1,0:T(8,128)(2,1)} %get-tuple-element.71), channel_id=1, source_target_pairs={{0,8},{2,10},{4,12},{6,14},{8,0},{10,2},{12,4},{14,6},{16,24},{18,... | collective-permute-start | bytes 405512 | tf_op jit(solution)/shard_map/ppermute | solution.py:397
  11.9 2.5 %collective-permute-start.12 = (bf16[264,256]{1,0:T(8,128)(2,1)}, bf16[264,256]{1,0:T(8,128)(2,1)S(1)}, u32[]{:S(2)}, u32[]{:S(2)}) collective-permute-start(bf16[264,256]{1,0:T(8,128)(2,1)} %get-tuple-element.73), channel_id=1, source_target_pairs={{0,12},{2,14},{4,8},{6,10},{8,4},{10,6},{12,0},{14,2},{16,28},{18,... | collective-permute-start | bytes 405512 | tf_op jit(solution)/shard_map/ppermute | solution.py:397
  18.6 3.8 %collective-permute-start = (bf16[264,256]{1,0:T(8,128)(2,1)S(1)}, bf16[264,256]{1,0:T(8,128)(2,1)S(1)}, u32[]{:S(2)}, u32[]{:S(2)}) collective-permute-start(bf16[264,256]{1,0:T(8,128)(2,1)S(1)} %get-tuple-element.60), channel_id=1, source_target_pairs={{0,2},{2,0},{4,6},{6,4},{8,10},{10,8},{12,14},{14,12},{16,18},{18,... | collective-permute-start | bytes 405512 | tf_op jit(solution)/shard_map/ppermute | solution.py:397
  26.3 3.1 %collective-permute-start.14 = (bf16[4,128,256]{2,1,0:T(8,128)(2,1)S(1)}, bf16[4,128,256]{2,1,0:T(8,128)(2,1)S(1)}, u32[]{:S(2)}, u32[]{:S(2)}) collective-permute-start(bf16[4,128,256]{2,1,0:T(8,128)(2,1)S(1)} %get-tuple-element.75), channel_id=1, source_target_pairs={{0,16},{2,18},{4,20},{6,22},{8,24},{10,26},{12,28},{14,30},{16,0},... | collective-permute-start | bytes 786440 | tf_op jit(solution)/shard_map/ppermute | solution.py:397
  29.6 2.0 %collective-permute-start.4 = (bf16[264,256]{1,0:T(8,128)(2,1)S(1)}, bf16[264,256]{1,0:T(8,128)(2,1)S(1)}, u32[]{:S(2)}, u32[]{:S(2)}) collective-permute-start(bf16[264,256]{1,0:T(8,128)(2,1)S(1)} %get-tuple-element.64), channel_id=1, source_target_pairs={{0,10},{2,8},{4,14},{6,12},{8,2},{10,0},{12,6},{14,4},{16,26},{18,... | collective-permute-start | bytes 405512 | tf_op jit(solution)/shard_map/ppermute | solution.py:397
  32.4 2.6 %collective-permute-start.6 = (bf16[264,256]{1,0:T(8,128)(2,1)S(1)}, bf16[264,256]{1,0:T(8,128)(2,1)S(1)}, u32[]{:S(2)}, u32[]{:S(2)}) collective-permute-start(bf16[264,256]{1,0:T(8,128)(2,1)S(1)} %get-tuple-element.66), channel_id=1, source_target_pairs={{0,14},{2,12},{4,10},{6,8},{8,6},{10,4},{12,2},{14,0},{16,30},{18,... | collective-permute-start | bytes 405512 | tf_op jit(solution)/shard_map/ppermute | solution.py:397
  36.0 7.6 %collective-permute-done.4.refs_5_ = bf16[264,256]{1,0:T(8,128)(2,1)S(1)} collective-permute-done((bf16[264,256]{1,0:T(8,128)(2,1)S(1)}, bf16[264,256]{1,0:T(8,128)(2,1)S(1)}, u32[]{:S(2)}, u32[]{:S(2)}) %collective-permute-start.4) | collective-permute-done | bytes 135200 | tf_op jit(solution)/shard_map/ppermute | solution.py:397
  45.2 5.9 %collective-permute-done.6.refs_7_ = bf16[264,256]{1,0:T(8,128)(2,1)S(1)} collective-permute-done((bf16[264,256]{1,0:T(8,128)(2,1)S(1)}, bf16[264,256]{1,0:T(8,128)(2,1)S(1)}, u32[]{:S(2)}, u32[]{:S(2)}) %collective-permute-start.6) | collective-permute-done | bytes 135200 | tf_op jit(solution)/shard_map/ppermute | solution.py:397
  66.4 1.7 %collective-permute-start.31 = (bf16[256,256]{1,0:T(8,128)(2,1)S(1)}, bf16[256,256]{1,0:T(8,128)(2,1)S(1)}, u32[]{:S(2)}, u32[]{:S(2)}) collective-permute-start(bf16[256,256]{1,0:T(8,128)(2,1)S(1)} %get-tuple-element.94), channel_id=1, source_target_pairs={{0,4},{2,6},{4,0},{6,2},{8,12},{10,14},{12,8},{14,10},{16,20},{18,... | collective-permute-start | bytes 393224 | tf_op jit(solution)/shard_map/ppermute | solution.py:397
  69.6 1.8 %collective-permute-start.23 = (bf16[128,512]{1,0:T(8,128)(2,1)S(1)}, bf16[128,512]{1,0:T(8,128)(2,1)S(1)}, u32[]{:S(2)}, u32[]{:S(2)}) collective-permute-start(bf16[128,512]{1,0:T(8,128)(2,1)S(1)} %shard_map.158.refs_0_), channel_id=1, source_target_pairs={{0,8},{2,10},{4,12},{6,14},{8,0},{10,2},{12,4},{14,6},{16,24},{18,... | collective-permute-start | bytes 393224 | tf_op jit(solution)/shard_map/ppermute | solution.py:397
  71.3 2.8 %collective-permute-done.31.refs_10_ = bf16[256,256]{1,0:T(8,128)(2,1)S(1)} collective-permute-done((bf16[256,256]{1,0:T(8,128)(2,1)S(1)}, bf16[256,256]{1,0:T(8,128)(2,1)S(1)}, u32[]{:S(2)}, u32[]{:S(2)}) %collective-permute-start.31) | collective-permute-done | bytes 131104 | tf_op jit(solution)/shard_map/ppermute | solution.py:397
  74.2 2.4 %collective-permute-start.33 = (bf16[256,256]{1,0:T(8,128)(2,1)S(1)}, bf16[256,256]{1,0:T(8,128)(2,1)S(1)}, u32[]{:S(2)}, u32[]{:S(2)}) collective-permute-start(bf16[256,256]{1,0:T(8,128)(2,1)S(1)} %get-tuple-element.96), channel_id=1, source_target_pairs={{0,8},{2,10},{4,12},{6,14},{8,0},{10,2},{12,4},{14,6},{16,24},{18,... | collective-permute-start | bytes 393224 | tf_op jit(solution)/shard_map/ppermute | solution.py:397
  76.9 3.3 %collective-permute-done.23.refs_1_ = bf16[128,512]{1,0:T(8,128)(2,1)S(1)} collective-permute-done((bf16[128,512]{1,0:T(8,128)(2,1)S(1)}, bf16[128,512]{1,0:T(8,128)(2,1)S(1)}, u32[]{:S(2)}, u32[]{:S(2)}) %collective-permute-start.23) | collective-permute-done | bytes 131104 | tf_op jit(solution)/shard_map/ppermute | solution.py:397
  80.2 2.6 %collective-permute-start.35 = (bf16[256,256]{1,0:T(8,128)(2,1)S(1)}, bf16[256,256]{1,0:T(8,128)(2,1)S(1)}, u32[]{:S(2)}, u32[]{:S(2)}) collective-permute-start(bf16[256,256]{1,0:T(8,128)(2,1)S(1)} %get-tuple-element.98), channel_id=1, source_target_pairs={{0,12},{2,14},{4,8},{6,10},{8,4},{10,6},{12,0},{14,2},{16,28},{18,... | collective-permute-start | bytes 393224 | tf_op jit(solution)/shard_map/ppermute | solution.py:397
  82.8 2.1 %collective-permute-done.28.first.refs_6_ = bf16[4,128,256]{2,1,0:T(8,128)(2,1)S(1)} collective-permute-done((bf16[4,128,256]{2,1,0:T(8,128)(2,1)S(1)}, bf16[4,128,256]{2,1,0:T(8,128)(2,1)S(1)}, u32[]{:S(2)}, u32[]{:S(2)}) %collective-permute-start.28) | collective-permute-done | bytes 262176 | tf_op jit(solution)/shard_map/ppermute | solution.py:397
  84.9 4.1 %collective-permute-done.29.second.refs_7_ = bf16[4,128,256]{2,1,0:T(8,128)(2,1)S(1)} collective-permute-done((bf16[4,128,256]{2,1,0:T(8,128)(2,1)S(1)}, bf16[4,128,256]{2,1,0:T(8,128)(2,1)S(1)}, u32[]{:S(2)}, u32[]{:S(2)}) %collective-permute-start.29) | collective-permute-done | bytes 262176 | tf_op jit(solution)/shard_map/ppermute | solution.py:397
  89.1 4.4 %collective-permute-start.24 = (bf16[128,512]{1,0:T(8,128)(2,1)S(1)}, bf16[128,512]{1,0:T(8,128)(2,1)S(1)}, u32[]{:S(2)}, u32[]{:S(2)}) collective-permute-start(bf16[128,512]{1,0:T(8,128)(2,1)S(1)} %shard_map.159.refs_0_), channel_id=1, source_target_pairs={{0,16},{2,18},{4,20},{6,22},{8,24},{10,26},{12,28},{14,30},{16,0},... | collective-permute-start | bytes 393224 | tf_op jit(solution)/shard_map/ppermute | solution.py:397
  94.8 4.4 %collective-permute-start.38 = (bf16[256,256]{1,0:T(8,128)(2,1)S(1)}, bf16[256,256]{1,0:T(8,128)(2,1)S(1)}, u32[]{:S(2)}, u32[]{:S(2)}) collective-permute-start(bf16[256,256]{1,0:T(8,128)(2,1)S(1)} %get-tuple-element.102), channel_id=1, source_target_pairs={{0,4},{2,6},{4,0},{6,2},{8,12},{10,14},{12,8},{14,10},{16,20},{18,... | collective-permute-start | bytes 393224 | tf_op jit(solution)/shard_map/ppermute | solution.py:397
  100.7 3.0 %collective-permute-done.36.refs_15_ = bf16[256,256]{1,0:T(8,128)(2,1)S(1)} collective-permute-done((bf16[256,256]{1,0:T(8,128)(2,1)S(1)}, bf16[256,256]{1,0:T(8,128)(2,1)S(1)}, u32[]{:S(2)}, u32[]{:S(2)}) %collective-permute-start.36) | collective-permute-done | bytes 131104 | tf_op jit(solution)/shard_map/ppermute | solution.py:397
  105.5 4.2 %collective-permute-start.43 = (bf16[256,256]{1,0:T(8,128)(2,1)S(1)}, bf16[256,256]{1,0:T(8,128)(2,1)S(1)}, u32[]{:S(2)}, u32[]{:S(2)}) collective-permute-start(bf16[256,256]{1,0:T(8,128)(2,1)S(1)} %get-tuple-element.107), channel_id=1, source_target_pairs={{0,14},{2,12},{4,10},{6,8},{8,6},{10,4},{12,2},{14,0},{16,30},{18,... | collective-permute-start | bytes 393224 | tf_op jit(solution)/shard_map/ppermute | solution.py:397
  110.1 4.3 %collective-permute-start.26 = (bf16[128,512]{1,0:T(8,128)(2,1)S(1)}, bf16[128,512]{1,0:T(8,128)(2,1)S(1)}, u32[]{:S(2)}, u32[]{:S(2)}) collective-permute-start(bf16[128,512]{1,0:T(8,128)(2,1)S(1)} %shard_map.160.refs_0_), channel_id=1, source_target_pairs={{0,4},{2,6},{4,0},{6,2},{8,12},{10,14},{12,8},{14,10},{16,20},{18,... | collective-permute-start | bytes 393224 | tf_op jit(solution)/shard_map/ppermute | solution.py:397
  117.1 2.2 %shard_map.167 = bf16[8,128,256]{2,1,0:T(8,128)(2,1)} custom-call(s32[16]{0:T(128)S(1)} %copy-done.12, s32[16]{0:T(128)S(1)} %copy-done.13, s32[32]{0:T(128)S(1)} %copy-done.9, bf16[16,128,128]{2,1,0:T(8,128)(2,1)S(1)} %copy-done.1, bf16[4,128,256]{2,1,0:T(8,128)(2,1)S(1)} %shard_map.162.refs_3_.first.refs_4_, ...), custom_call_target="tpu_custom_call" | custom-call | flops 1048576 | bytes 1048576 | tf_op jit(solution)/shard_map/pallas_call | solution.py:29
  (115 shorter events, 40.4 us)
Async XLA Ops:
  8.4 10.1 %collective-permute-start.9 = (bf16[264,256]{1,0:T(8,128)(2,1)}, bf16[264,256]{1,0:T(8,128)(2,1)S(1)}, u32[]{:S(2)}, u32[]{:S(2)}) collective-permute-start(bf16[264,256]{1,0:T(8,128)(2,1)} %get-tuple-element.70), channel_id=1, source_target_pairs={{0,6},{2,4},{4,2},{6,0},{8,14},{10,12},{12,10},{14,8},{16,22},{18,... | collective-permute-start | bytes 405512 | tf_op jit(solution)/shard_map/ppermute | solution.py:397
  8.5 13.9 %collective-permute-start.10 = (bf16[264,256]{1,0:T(8,128)(2,1)}, bf16[264,256]{1,0:T(8,128)(2,1)S(1)}, u32[]{:S(2)}, u32[]{:S(2)}) collective-permute-start(bf16[264,256]{1,0:T(8,128)(2,1)} %get-tuple-element.71), channel_id=1, source_target_pairs={{0,8},{2,10},{4,12},{6,14},{8,0},{10,2},{12,4},{14,6},{16,24},{18,... | collective-permute-start | bytes 405512 | tf_op jit(solution)/shard_map/ppermute | solution.py:397
  10.5 11.9 %collective-permute-start.11 = (bf16[264,256]{1,0:T(8,128)(2,1)}, bf16[264,256]{1,0:T(8,128)(2,1)S(1)}, u32[]{:S(2)}, u32[]{:S(2)}) collective-permute-start(bf16[264,256]{1,0:T(8,128)(2,1)} %get-tuple-element.72), channel_id=1, source_target_pairs={{0,10},{2,8},{4,14},{6,12},{8,2},{10,0},{12,6},{14,4},{16,26},{18,... | collective-permute-start | bytes 405512 | tf_op jit(solution)/shard_map/ppermute | solution.py:397
  11.9 12.1 %collective-permute-start.12 = (bf16[264,256]{1,0:T(8,128)(2,1)}, bf16[264,256]{1,0:T(8,128)(2,1)S(1)}, u32[]{:S(2)}, u32[]{:S(2)}) collective-permute-start(bf16[264,256]{1,0:T(8,128)(2,1)} %get-tuple-element.73), channel_id=1, source_target_pairs={{0,12},{2,14},{4,8},{6,10},{8,4},{10,6},{12,0},{14,2},{16,28},{18,... | collective-permute-start | bytes 405512 | tf_op jit(solution)/shard_map/ppermute | solution.py:397
  14.4 10.9 %collective-permute-start.13 = (bf16[264,256]{1,0:T(8,128)(2,1)}, bf16[264,256]{1,0:T(8,128)(2,1)S(1)}, u32[]{:S(2)}, u32[]{:S(2)}) collective-permute-start(bf16[264,256]{1,0:T(8,128)(2,1)} %get-tuple-element.74), channel_id=1, source_target_pairs={{0,14},{2,12},{4,10},{6,8},{8,6},{10,4},{12,2},{14,0},{16,30},{18,... | collective-permute-start | bytes 405512 | tf_op jit(solution)/shard_map/ppermute | solution.py:397
  18.6 10.8 %collective-permute-start = (bf16[264,256]{1,0:T(8,128)(2,1)S(1)}, bf16[264,256]{1,0:T(8,128)(2,1)S(1)}, u32[]{:S(2)}, u32[]{:S(2)}) collective-permute-start(bf16[264,256]{1,0:T(8,128)(2,1)S(1)} %get-tuple-element.60), channel_id=1, source_target_pairs={{0,2},{2,0},{4,6},{6,4},{8,10},{10,8},{12,14},{14,12},{16,18},{18,... | collective-permute-start | bytes 405512 | tf_op jit(solution)/shard_map/ppermute | solution.py:397
  26.3 24.8 %collective-permute-start.14 = (bf16[4,128,256]{2,1,0:T(8,128)(2,1)S(1)}, bf16[4,128,256]{2,1,0:T(8,128)(2,1)S(1)}, u32[]{:S(2)}, u32[]{:S(2)}) collective-permute-start(bf16[4,128,256]{2,1,0:T(8,128)(2,1)S(1)} %get-tuple-element.75), channel_id=1, source_target_pairs={{0,16},{2,18},{4,20},{6,22},{8,24},{10,26},{12,28},{14,30},{16,0},... | collective-permute-start | bytes 786440 | tf_op jit(solution)/shard_map/ppermute | solution.py:397
  29.4 23.2 %collective-permute-start.16 = (bf16[4,128,256]{2,1,0:T(8,128)(2,1)S(1)}, bf16[4,128,256]{2,1,0:T(8,128)(2,1)S(1)}, u32[]{:S(2)}, u32[]{:S(2)}) collective-permute-start(bf16[4,128,256]{2,1,0:T(8,128)(2,1)S(1)} %get-tuple-element.81), channel_id=1, source_target_pairs={{0,16},{2,18},{4,20},{6,22},{8,24},{10,26},{12,28},{14,30},{16,0},... | collective-permute-start | bytes 786440 | tf_op jit(solution)/shard_map/ppermute | solution.py:397
  29.6 14.0 %collective-permute-start.4 = (bf16[264,256]{1,0:T(8,128)(2,1)S(1)}, bf16[264,256]{1,0:T(8,128)(2,1)S(1)}, u32[]{:S(2)}, u32[]{:S(2)}) collective-permute-start(bf16[264,256]{1,0:T(8,128)(2,1)S(1)} %get-tuple-element.64), channel_id=1, source_target_pairs={{0,10},{2,8},{4,14},{6,12},{8,2},{10,0},{12,6},{14,4},{16,26},{18,... | collective-permute-start | bytes 405512 | tf_op jit(solution)/shard_map/ppermute | solution.py:397
  31.6 13.6 %collective-permute-start.5 = (bf16[264,256]{1,0:T(8,128)(2,1)S(1)}, bf16[264,256]{1,0:T(8,128)(2,1)S(1)}, u32[]{:S(2)}, u32[]{:S(2)}) collective-permute-start(bf16[264,256]{1,0:T(8,128)(2,1)S(1)} %get-tuple-element.65), channel_id=1, source_target_pairs={{0,12},{2,14},{4,8},{6,10},{8,4},{10,6},{12,0},{14,2},{16,28},{18,... | collective-permute-start | bytes 405512 | tf_op jit(solution)/shard_map/ppermute | solution.py:397
  32.4 18.7 %collective-permute-start.6 = (bf16[264,256]{1,0:T(8,128)(2,1)S(1)}, bf16[264,256]{1,0:T(8,128)(2,1)S(1)}, u32[]{:S(2)}, u32[]{:S(2)}) collective-permute-start(bf16[264,256]{1,0:T(8,128)(2,1)S(1)} %get-tuple-element.66), channel_id=1, source_target_pairs={{0,14},{2,12},{4,10},{6,8},{8,6},{10,4},{12,2},{14,0},{16,30},{18,... | collective-permute-start | bytes 405512 | tf_op jit(solution)/shard_map/ppermute | solution.py:397
  63.5 21.4 %collective-permute-start.28 = (bf16[4,128,256]{2,1,0:T(8,128)(2,1)S(1)}, bf16[4,128,256]{2,1,0:T(8,128)(2,1)S(1)}, u32[]{:S(2)}, u32[]{:S(2)}) collective-permute-start(bf16[4,128,256]{2,1,0:T(8,128)(2,1)S(1)} %shard_map.162.refs_3_.first.refs_4_), channel_id=1, source_target_pairs={{0,16},{2,18},{4,20},{6,22},{8,24},{10,26},{12,28},{14,30},{16,0},... | collective-permute-start | bytes 786440 | tf_op jit(solution)/shard_map/ppermute | solution.py:397
  65.0 24.0 %collective-permute-start.29 = (bf16[4,128,256]{2,1,0:T(8,128)(2,1)S(1)}, bf16[4,128,256]{2,1,0:T(8,128)(2,1)S(1)}, u32[]{:S(2)}, u32[]{:S(2)}) collective-permute-start(bf16[4,128,256]{2,1,0:T(8,128)(2,1)S(1)} %shard_map.163.refs_4_.second.refs_5_), channel_id=1, source_target_pairs={{0,16},{2,18},{4,20},{6,22},{8,24},{10,26},{12,28},{14,30},{16,0},... | collective-permute-start | bytes 786440 | tf_op jit(solution)/shard_map/ppermute | solution.py:397
  69.6 10.6 %collective-permute-start.23 = (bf16[128,512]{1,0:T(8,128)(2,1)S(1)}, bf16[128,512]{1,0:T(8,128)(2,1)S(1)}, u32[]{:S(2)}, u32[]{:S(2)}) collective-permute-start(bf16[128,512]{1,0:T(8,128)(2,1)S(1)} %shard_map.158.refs_0_), channel_id=1, source_target_pairs={{0,8},{2,10},{4,12},{6,14},{8,0},{10,2},{12,4},{14,6},{16,24},{18,... | collective-permute-start | bytes 393224 | tf_op jit(solution)/shard_map/ppermute | solution.py:397
  74.2 20.0 %collective-permute-start.33 = (bf16[256,256]{1,0:T(8,128)(2,1)S(1)}, bf16[256,256]{1,0:T(8,128)(2,1)S(1)}, u32[]{:S(2)}, u32[]{:S(2)}) collective-permute-start(bf16[256,256]{1,0:T(8,128)(2,1)S(1)} %get-tuple-element.96), channel_id=1, source_target_pairs={{0,8},{2,10},{4,12},{6,14},{8,0},{10,2},{12,4},{14,6},{16,24},{18,... | collective-permute-start | bytes 393224 | tf_op jit(solution)/shard_map/ppermute | solution.py:397
  76.6 18.3 %collective-permute-start.34 = (bf16[256,256]{1,0:T(8,128)(2,1)S(1)}, bf16[256,256]{1,0:T(8,128)(2,1)S(1)}, u32[]{:S(2)}, u32[]{:S(2)}) collective-permute-start(bf16[256,256]{1,0:T(8,128)(2,1)S(1)} %get-tuple-element.97), channel_id=1, source_target_pairs={{0,10},{2,8},{4,14},{6,12},{8,2},{10,0},{12,6},{14,4},{16,26},{18,... | collective-permute-start | bytes 393224 | tf_op jit(solution)/shard_map/ppermute | solution.py:397
  80.2 19.1 %collective-permute-start.35 = (bf16[256,256]{1,0:T(8,128)(2,1)S(1)}, bf16[256,256]{1,0:T(8,128)(2,1)S(1)}, u32[]{:S(2)}, u32[]{:S(2)}) collective-permute-start(bf16[256,256]{1,0:T(8,128)(2,1)S(1)} %get-tuple-element.98), channel_id=1, source_target_pairs={{0,12},{2,14},{4,8},{6,10},{8,4},{10,6},{12,0},{14,2},{16,28},{18,... | collective-permute-start | bytes 393224 | tf_op jit(solution)/shard_map/ppermute | solution.py:397
  84.9 18.8 %collective-permute-start.36 = (bf16[256,256]{1,0:T(8,128)(2,1)S(1)}, bf16[256,256]{1,0:T(8,128)(2,1)S(1)}, u32[]{:S(2)}, u32[]{:S(2)}) collective-permute-start(bf16[256,256]{1,0:T(8,128)(2,1)S(1)} %get-tuple-element.99), channel_id=1, source_target_pairs={{0,14},{2,12},{4,10},{6,8},{8,6},{10,4},{12,2},{14,0},{16,30},{18,... | collective-permute-start | bytes 393224 | tf_op jit(solution)/shard_map/ppermute | solution.py:397
  89.1 14.7 %collective-permute-start.24 = (bf16[128,512]{1,0:T(8,128)(2,1)S(1)}, bf16[128,512]{1,0:T(8,128)(2,1)S(1)}, u32[]{:S(2)}, u32[]{:S(2)}) collective-permute-start(bf16[128,512]{1,0:T(8,128)(2,1)S(1)} %shard_map.159.refs_0_), channel_id=1, source_target_pairs={{0,16},{2,18},{4,20},{6,22},{8,24},{10,26},{12,28},{14,30},{16,0},... | collective-permute-start | bytes 393224 | tf_op jit(solution)/shard_map/ppermute | solution.py:397
  94.8 10.7 %collective-permute-start.38 = (bf16[256,256]{1,0:T(8,128)(2,1)S(1)}, bf16[256,256]{1,0:T(8,128)(2,1)S(1)}, u32[]{:S(2)}, u32[]{:S(2)}) collective-permute-start(bf16[256,256]{1,0:T(8,128)(2,1)S(1)} %get-tuple-element.102), channel_id=1, source_target_pairs={{0,4},{2,6},{4,0},{6,2},{8,12},{10,14},{12,8},{14,10},{16,20},{18,... | collective-permute-start | bytes 393224 | tf_op jit(solution)/shard_map/ppermute | solution.py:397
  99.3 10.4 %collective-permute-start.39 = (bf16[256,256]{1,0:T(8,128)(2,1)S(1)}, bf16[256,256]{1,0:T(8,128)(2,1)S(1)}, u32[]{:S(2)}, u32[]{:S(2)}) collective-permute-start(bf16[256,256]{1,0:T(8,128)(2,1)S(1)} %get-tuple-element.103), channel_id=1, source_target_pairs={{0,6},{2,4},{4,2},{6,0},{8,14},{10,12},{12,10},{14,8},{16,22},{18,... | collective-permute-start | bytes 393224 | tf_op jit(solution)/shard_map/ppermute | solution.py:397
  103.7 10.7 %collective-permute-start.41 = (bf16[256,256]{1,0:T(8,128)(2,1)S(1)}, bf16[256,256]{1,0:T(8,128)(2,1)S(1)}, u32[]{:S(2)}, u32[]{:S(2)}) collective-permute-start(bf16[256,256]{1,0:T(8,128)(2,1)S(1)} %get-tuple-element.105), channel_id=1, source_target_pairs={{0,10},{2,8},{4,14},{6,12},{8,2},{10,0},{12,6},{14,4},{16,26},{18,... | collective-permute-start | bytes 393224 | tf_op jit(solution)/shard_map/ppermute | solution.py:397
  104.0 13.1 %collective-permute-start.42 = (bf16[256,256]{1,0:T(8,128)(2,1)S(1)}, bf16[256,256]{1,0:T(8,128)(2,1)S(1)}, u32[]{:S(2)}, u32[]{:S(2)}) collective-permute-start(bf16[256,256]{1,0:T(8,128)(2,1)S(1)} %get-tuple-element.106), channel_id=1, source_target_pairs={{0,12},{2,14},{4,8},{6,10},{8,4},{10,6},{12,0},{14,2},{16,28},{18,... | collective-permute-start | bytes 393224 | tf_op jit(solution)/shard_map/ppermute | solution.py:397
  105.5 11.6 %collective-permute-start.43 = (bf16[256,256]{1,0:T(8,128)(2,1)S(1)}, bf16[256,256]{1,0:T(8,128)(2,1)S(1)}, u32[]{:S(2)}, u32[]{:S(2)}) collective-permute-start(bf16[256,256]{1,0:T(8,128)(2,1)S(1)} %get-tuple-element.107), channel_id=1, source_target_pairs={{0,14},{2,12},{4,10},{6,8},{8,6},{10,4},{12,2},{14,0},{16,30},{18,... | collective-permute-start | bytes 393224 | tf_op jit(solution)/shard_map/ppermute | solution.py:397
  (35 other events, 208.3 us)
